TPU v7x, 256 devices: a whole 4x4x8 slice. The times are simulated.
256 devices in a mesh: frame: 8 (over z), tile: 32 (over x, y, core).
Axes of the slice: x: 4, y: 4, z: 8, core: 2. Of those that a mesh axis runs over, the one named last changes fastest.
Arguments:
- kspace_samples: bfloat16 [16, 128, 32, 128], P('frame', 'tile'), may hold values from -6 to 6
- density: bfloat16 [16, 128, 128], P('frame', 'tile'), may hold values from 0.796875 to 8
- sample_frac: bfloat16 [16, 128, 3, 128], P('frame', 'tile'), may hold values from 0 to 1
- row_offsets: int32 [16, 128, 128], P('frame', 'tile'), may hold values from 0 to 2
- depth_base: int32 [16, 128, 128], P('frame', 'tile'), may hold values from 0 to 127
- block_base: int32 [16, 128, 2], P('frame', 'tile'), may hold values from 0 to 127, as said below
- coil_maps: bfloat16 [16, 2, 128, 128, 128], P(None, None, 'tile'), may hold values from -1.5 to 1.5
- estimate: float32 [16, 2, 128, 128, 128], P('frame', None, 'tile'), may hold values from -6 to 6
Outputs:
- updated: float32 [16, 2, 128, 128, 128], P('frame', None, 'tile')
Inputs may be any that keep to these rules, and one draw needn't show every extreme that they name: `block_base`: block b of a frame is held by tile index b // 4. Its kx planes are xb .. xb + 5 mod 128, and tile number p holds planes p * 4 .. p * 4 + 3. In every frame, at most 1 block of one tile index touch any one tile, and some tile is touched by exactly 1 block of every tile index.
All inputs are finite; a program needn't handle non-finite values.
Results may differ from a plain program's by a relative error of at most 0.0095.
Values may be sent and summed in bfloat16 or wider, within the bound.
A program may use at most 128 MiB of HBM per device.

v0:
```python
import functools
import math

import jax
import jax.numpy as jnp
import numpy as np
from jax import lax
from jax.experimental import pallas as pl
from jax.experimental.pallas import tpu as pltpu
from jax.sharding import PartitionSpec as P

MESH = pl.DeviceIdType.MESH
BETA = 13.9
EPS = 0.05
LAMBDA_TV = 0.3
TAPS = 6
POWERS = 40

ROW_WX, ROW_XB, ROW_WZ, ROW_WY, ROW_YB, ROW_ZB, ROWS = 32, 38, 40, 48, 54, 55, 56


def kaiser_coefficients():
    terms, term = [], 1.0
    for power in range(POWERS):
        if power:
            term *= BETA * BETA / 4.0 / (power * power)
        terms.append(term)
    total = sum(terms)
    return [term / total for term in terms]


def kaiser(offset, fraction):
    distance = (offset - 2.0 - fraction) * (1.0 / 3.0)
    inside = jnp.maximum(1.0 - distance * distance, 0.0)
    terms = kaiser_coefficients()
    result = jnp.full_like(inside, terms[-1])
    for term in reversed(terms[:-1]):
        result = result * inside + term
    return result


def dft_tables(size):
    index = np.arange(size)
    angles = (index[:, None] * index[None, :] % size) * (2.0 * np.pi / size)
    cosine, sine = np.cos(angles), np.sin(angles)
    right = np.block([[cosine, sine], [-sine, cosine]])
    left = np.block([[cosine, -sine], [sine, cosine]])
    return right.astype(np.float32), left.astype(np.float32)


def message_kernel(samples_ref, density_ref, frac_ref, shift_ref, depth_ref, base_ref, out_ref, lines_ref):
    frames, blocks, channels, lanes = samples_ref.shape
    coils = channels // 2
    grid_mask = 127
    row = lax.broadcasted_iota(jnp.int32, (8, lanes), 0)
    offset = row.astype(jnp.float32)
    for frame in range(frames):
        for block in range(blocks):
            slot = frame * blocks + block
            lines_ref[slot] = samples_ref[frame, block].astype(jnp.float32) * density_ref[frame, block : block + 1].astype(jnp.float32)
            taps = [
                jnp.where(row < TAPS, kaiser(offset, frac_ref[frame, block, axis : axis + 1].astype(jnp.float32)), 0.0)
                for axis in range(3)
            ]
            plane = base_ref[frame, block, 0].astype(jnp.float32)
            first_row = (shift_ref[frame, block : block + 1] + base_ref[frame, block, 1]) & grid_mask
            first_cell = depth_ref[frame, block : block + 1]
            group_x = jnp.where(row == ROW_XB - ROW_WX, plane, taps[0])
            group_y = jnp.where(row == ROW_YB - ROW_WY, first_row.astype(jnp.float32), taps[1])
            group_y = jnp.where(row == ROW_ZB - ROW_WY, first_cell.astype(jnp.float32), group_y)
            out_ref[frame, block, 0:coils] = lines_ref[slot, pl.ds(0, coils, stride=2), :].astype(jnp.bfloat16)
            out_ref[frame, block, coils:channels] = lines_ref[slot, pl.ds(1, coils, stride=2), :].astype(jnp.bfloat16)
            out_ref[frame, block, ROW_WX : ROW_WX + 16] = jnp.concatenate([group_x, taps[2]], axis=0).astype(jnp.bfloat16)
            out_ref[frame, block, ROW_WY : ROW_WY + 8] = group_y.astype(jnp.bfloat16)


def row_tables(image_rows, grid, lanes):
    angle_of = lambda index: (index % grid).astype(jnp.float32) * (2.0 * math.pi / grid)
    turn = angle_of(image_rows[:, None] * jnp.arange(lanes)[None, :])
    step = jnp.broadcast_to(angle_of(jnp.arange(TAPS)[:, None] * image_rows[None, :])[:, :, None], (TAPS, image_rows.shape[0], lanes))
    angles = jnp.concatenate([turn[None], step], axis=0)
    cosine, sine = jnp.cos(angles), jnp.sin(angles)
    rows = lambda upper, lower: jnp.concatenate([upper, lower], axis=1)
    return jnp.concatenate(
        [rows(cosine, sine)[:1], rows(sine, cosine)[:1], rows(cosine, cosine)[1:], rows(-sine, sine)[1:]], axis=0
    )


def block_messages(kspace_samples, density, sample_frac, row_offsets, depth_base, block_base):
    frames, blocks, channels, lanes = kspace_samples.shape
    vmem, smem = pl.BlockSpec(memory_space=pltpu.VMEM), pl.BlockSpec(memory_space=pltpu.SMEM)
    return pl.pallas_call(
        message_kernel,
        out_shape=jax.ShapeDtypeStruct((frames, blocks, ROWS, lanes), jnp.bfloat16),
        in_specs=[vmem] * 5 + [smem],
        out_specs=vmem,
        scratch_shapes=[pltpu.VMEM((frames * blocks, channels, lanes), jnp.float32)],
        name="message",
    )(kspace_samples, density, sample_frac, row_offsets, depth_base, block_base)


def gather_kernel(side, msg_ref, out_ref, send_sem, recv_sem, own_sem):
    tile = lax.axis_index("tile")
    core, chip = tile % 2, tile // 2
    chip_x, chip_y = chip // side, chip % side
    first = chip_x + core * (chip_y - chip_x)
    other = chip_y + core * (chip_x - chip_y)
    first_step = 2 * side - (2 * side - 2) * core
    other_step = 2 + (2 * side - 2) * core

    def at(along, across):
        return ((first + along + side) % side) * first_step + ((other + across + side) % side) * other_step + core

    partner = tile + 1 - 2 * core
    neighbours = [at(1, 0), at(-1, 0), at(0, 1), at(0, -1), partner]

    barrier = pltpu.get_barrier_semaphore()
    for device in neighbours:
        pl.semaphore_signal(barrier, inc=1, device_id={"tile": device}, device_id_type=MESH)
    pl.semaphore_wait(barrier, len(neighbours))

    def whole(number, slot, target, own=False):
        return pltpu.make_async_remote_copy(
            src_ref=msg_ref if own else out_ref.at[slot],
            dst_ref=out_ref.at[slot],
            send_sem=send_sem.at[number],
            recv_sem=recv_sem.at[number],
            device_id={"tile": target},
            device_id_type=MESH,
        )

    def part(number, slot, frame, target):
        return pltpu.make_async_remote_copy(
            src_ref=out_ref.at[slot, frame],
            dst_ref=out_ref.at[slot, frame],
            send_sem=send_sem.at[number],
            recv_sem=recv_sem.at[number],
            device_id={"tile": target},
            device_id_type=MESH,
        )

    copies = {0: whole(0, tile, at(1, 0), True), 1: whole(1, tile, at(-1, 0), True)}
    copies[2] = part(2, at(-1, 0), 0, at(1, 0))
    copies[3] = part(3, at(1, 0), 1, at(-1, 0))
    places = [0, -1, 1, 2]
    for index, along in enumerate(places):
        base = 4 + 4 * index
        copies[base] = whole(base, at(along, 0), at(0, 1), along == 0)
        copies[base + 1] = whole(base + 1, at(along, 0), at(0, -1), along == 0)
        copies[base + 2] = part(base + 2, at(along, -1), 0, at(0, 1))
        copies[base + 3] = part(base + 3, at(along, 1), 1, at(0, -1))
        for turn, across in enumerate(places):
            number = 20 + 4 * index + turn
            copies[number] = whole(number, at(along, across), partner, along == 0 and across == 0)

    def start(*numbers):
        for number in numbers:
            copies[number].start()

    def arrived(*numbers):
        for number in numbers:
            copies[number].wait_recv()

    own = pltpu.make_async_copy(msg_ref, out_ref.at[tile], own_sem)
    start(0, 1, 4, 5, 20)
    own.start()
    arrived(0)
    start(2, 8, 9, 24)
    arrived(1)
    start(3, 12, 13, 28)
    arrived(4)
    start(6, 21)
    arrived(5)
    start(7, 22)
    arrived(2, 3)
    start(16, 17, 32)
    for index in (1, 2, 3):
        base = 4 + 4 * index
        arrived(base)
        start(base + 2, 20 + 4 * index + 1)
        arrived(base + 1)
        start(base + 3, 20 + 4 * index + 2)
    for index in range(4):
        base = 4 + 4 * index
        arrived(base + 2, base + 3)
        start(20 + 4 * index + 3)
    arrived(*range(20, 36))
    for number in range(36):
        copies[number].wait_send()
    own.wait()


def gather_messages(message, tiles, side):
    return pl.pallas_call(
        functools.partial(gather_kernel, side),
        out_shape=jax.ShapeDtypeStruct((tiles,) + message.shape, message.dtype),
        in_specs=[pl.BlockSpec(memory_space=pltpu.VMEM)],
        out_specs=pl.BlockSpec(memory_space=pl.ANY),
        scratch_shapes=[
            pltpu.SemaphoreType.DMA((36,)),
            pltpu.SemaphoreType.DMA((36,)),
            pltpu.SemaphoreType.DMA(()),
        ],
        compiler_params=pltpu.CompilerParams(collective_id=0, has_side_effects=True),
        name="gather",
    )(message)


def grid_kernel(grid, coils, rows, blocks, scale, xb_ref, msg_ref, tables_ref, right_ref, left_ref, maps_ref, est_ref, out_ref, acc_ref):
    frame = pl.program_id(0)
    half_rows = rows * coils
    plane = 2 * half_rows
    per_tile = msg_ref.shape[2]

    def clear(step, carry):
        acc_ref[pl.ds(pl.multiple_of(step * 128, 128), 128), :] = jnp.zeros((128, grid), jnp.float32)
        return carry

    lax.fori_loop(0, grid * plane // 128, clear, 0, unroll=4)
    cells = lax.broadcasted_iota(jnp.int32, (8, 128), 0)

    def one_block(block, carry):
        tile, local = block // per_tile, block % per_tile
        real = msg_ref[tile, 0, local, 0:coils, :].astype(jnp.float32)
        imag = msg_ref[tile, 0, local, coils : 2 * coils, :].astype(jnp.float32)
        weights = msg_ref[tile, 0, local, ROW_WX : ROW_WX + 8, :].astype(jnp.float32)
        depth = msg_ref[tile, 0, local, ROW_WZ : ROW_WZ + 8, :].astype(jnp.float32)
        tail = msg_ref[tile, 0, local, ROW_WY : ROW_WY + 8, :].astype(jnp.float32)
        first_row = jnp.broadcast_to(tail[ROW_YB - ROW_WY : ROW_YB - ROW_WY + 1, :].astype(jnp.int32), (8, 128))
        first_cell = tail[ROW_ZB - ROW_WY : ROW_ZB - ROW_WY + 1, :].astype(jnp.int32)
        turn = jnp.take_along_axis(tables_ref[0], first_row, axis=1)
        swapped = jnp.take_along_axis(tables_ref[1], first_row, axis=1)
        sum_same = sum(tail[e : e + 1] * tables_ref[2 + e] for e in range(TAPS))
        sum_cross = sum(tail[e : e + 1] * tables_ref[2 + TAPS + e] for e in range(TAPS))
        phase = turn * sum_same + swapped * sum_cross
        reals = [real * phase[y : y + 1] - imag * phase[rows + y : rows + y + 1] for y in range(rows)]
        imags = [real * phase[rows + y : rows + y + 1] + imag * phase[y : y + 1] for y in range(rows)]
        field = jnp.concatenate(reals + imags, axis=0)
        lag0 = cells - first_cell
        pieces = []
        for group in range(grid // 8):
            lag = jnp.minimum((lag0 + group * 8) & (grid - 1), 7)
            pieces.append(jnp.take_along_axis(depth, lag, axis=0))
        spread = jnp.concatenate(pieces, axis=0).astype(jnp.bfloat16)
        left = jnp.concatenate([(field * weights[tap : tap + 1]).astype(jnp.bfloat16) for tap in range(TAPS)], axis=0)
        value = lax.dot_general(left, spread, (((1,), (1,)), ((), ())), preferred_element_type=jnp.float32)
        first_plane = xb_ref[frame, block]
        for tap in range(TAPS):
            start = pl.multiple_of(((first_plane + tap) & (grid - 1)) * plane, plane)
            acc_ref[pl.ds(start, plane), :] += value[tap * plane : (tap + 1) * plane]
        return carry

    lax.fori_loop(0, blocks, one_block, 0, unroll=4)

    right = right_ref[...]
    left = left_ref[...]
    for y in range(rows):
        out_ref[0, 0, y] = jnp.zeros((grid, grid), jnp.float32)
        out_ref[0, 1, y] = jnp.zeros((grid, grid), jnp.float32)

        def one_pair(pair, carry, y=y):
            coil = pair * 2
            lines = []
            for part in range(2):
                base = y * coils + coil + part
                re = acc_ref[pl.ds(base, grid, stride=plane), :]
                im = acc_ref[pl.ds(half_rows + base, grid, stride=plane), :]
                lines.append(jnp.concatenate([re, im], axis=1).astype(jnp.bfloat16))
            second = jnp.dot(jnp.concatenate(lines, axis=0), right, preferred_element_type=jnp.float32).astype(jnp.bfloat16)
            stacked = jnp.concatenate(
                [
                    jnp.concatenate([second[:grid, :grid], second[grid:, :grid]], axis=1),
                    jnp.concatenate([second[:grid, grid:], second[grid:, grid:]], axis=1),
                ],
                axis=0,
            )
            image = jnp.dot(left, stacked, preferred_element_type=jnp.float32)
            back_re = jnp.zeros((grid, grid), jnp.float32)
            back_im = jnp.zeros((grid, grid), jnp.float32)
            for part in range(2):
                image_re = image[:grid, part * grid : (part + 1) * grid]
                image_im = image[grid:, part * grid : (part + 1) * grid]
                map_re = maps_ref[coil + part, 0, y].astype(jnp.float32)
                map_im = maps_ref[coil + part, 1, y].astype(jnp.float32)
                back_re += map_re * image_re + map_im * image_im
                back_im += map_re * image_im - map_im * image_re
            out_ref[0, 0, y] += back_re
            out_ref[0, 1, y] += back_im
            return carry

        lax.fori_loop(0, coils // 2, one_pair, 0, unroll=8)
        out_ref[0, 0, y] = est_ref[0, 0, y] + scale * out_ref[0, 0, y]
        out_ref[0, 1, y] = est_ref[0, 1, y] + scale * out_ref[0, 1, y]


def half_step(gathered, first_plane, tables, coil_maps, estimate, scale):
    tiles, frames, per_tile = gathered.shape[:3]
    coils, _, rows, grid, _ = coil_maps.shape
    blocks = tiles * per_tile
    right, left = (jnp.asarray(table, jnp.bfloat16) for table in dft_tables(grid))
    once = pl.Buffered(1)
    return pl.pallas_call(
        functools.partial(grid_kernel, grid, coils, rows, blocks, scale),
        out_shape=jax.ShapeDtypeStruct(estimate.shape, jnp.float32),
        grid_spec=pltpu.PrefetchScalarGridSpec(
            num_scalar_prefetch=1,
            grid=(frames,),
            in_specs=[
                pl.BlockSpec((tiles, 1, per_tile, ROWS, 128), lambda f, s: (0, f, 0, 0, 0)),
                pl.BlockSpec(tables.shape, lambda f, s: (0, 0, 0), pipeline_mode=once),
                pl.BlockSpec((2 * grid, 2 * grid), lambda f, s: (0, 0), pipeline_mode=once),
                pl.BlockSpec((2 * grid, 2 * grid), lambda f, s: (0, 0), pipeline_mode=once),
                pl.BlockSpec(coil_maps.shape, lambda f, s: (0, 0, 0, 0, 0), pipeline_mode=once),
                pl.BlockSpec((1, 2, rows, grid, grid), lambda f, s: (f, 0, 0, 0, 0)),
            ],
            out_specs=pl.BlockSpec((1, 2, rows, grid, grid), lambda f, s: (f, 0, 0, 0, 0)),
            scratch_shapes=[pltpu.VMEM((grid * 2 * rows * coils, grid), jnp.float32)],
        ),
        compiler_params=pltpu.CompilerParams(vmem_limit_bytes=56 * 1024 * 1024),
        name="grid",
    )(first_plane, gathered, tables, right, left, coil_maps, estimate)


def on_device(
    kspace_samples, density, sample_frac, row_offsets, depth_base, block_base, coil_maps, estimate
):
    tile_count = lax.axis_size("tile")
    tile_here = lax.axis_index("tile")
    frame_here = lax.axis_index("frame")
    frames, per_tile, channels, samples = kspace_samples.shape
    coils = channels // 2
    grid = coil_maps.shape[3]
    rows = coil_maps.shape[2]
    scale = 1.0 / (8.0 * math.sqrt(per_tile * tile_count * samples))

    message = block_messages(kspace_samples, density, sample_frac, row_offsets, depth_base, block_base)
    gathered = gather_messages(message, tile_count, math.isqrt(tile_count // 2))

    first_plane = gathered[:, :, :, ROW_XB, 0].astype(jnp.int32)
    first_plane = jnp.moveaxis(first_plane, 1, 0).reshape(frames, tile_count * per_tile)
    tables = row_tables(tile_here * rows + jnp.arange(rows), grid, samples)
    half = half_step(gathered, first_plane, tables, coil_maps, estimate, scale)

    count = lax.axis_size("frame")
    forward = [(i, i + 1) for i in range(count - 1)]
    backward = [(target, source) for source, target in forward]
    low = lax.ppermute(half[-1:].astype(jnp.bfloat16), "frame", forward)
    high = lax.ppermute(half[:1].astype(jnp.bfloat16), "frame", backward)
    padded = jnp.concatenate([low.astype(jnp.float32), half, high.astype(jnp.float32)], axis=0)
    change = padded[1:] - padded[:-1]
    magnitude = jnp.sqrt(change[:, 0] * change[:, 0] + change[:, 1] * change[:, 1] + EPS * EPS)
    psi = change / magnitude[:, None]
    pair_index = frame_here * frames + jnp.arange(frames + 1) - 1
    valid = (pair_index >= 0) & (pair_index <= count * frames - 2)
    psi = jnp.where(valid[:, None, None, None, None], psi, 0.0)
    return half - LAMBDA_TV * (psi[:-1] - psi[1:])


def solution(mesh):
    in_specs = (
        P("frame", "tile", None, None),
        P("frame", "tile", None),
        P("frame", "tile", None, None),
        P("frame", "tile", None),
        P("frame", "tile", None),
        P("frame", "tile", None),
        P(None, None, "tile", None, None),
        P("frame", None, "tile", None, None),
    )
    out_specs = P("frame", None, "tile", None, None)
    return jax.shard_map(
        on_device, mesh=mesh, in_specs=in_specs, out_specs=out_specs, check_vma=False
    )
```

profile of v0, /device:TPU:96, one launch (start us, length us, event | category | flops | bytes accessed | tf_op | source)
XLA Modules:
  0.0 105.0 jit_solution(11461835585602220260)
XLA Ops:
  0.0 0.1 fusion.23
  0.1 1.4 %copy.19.base_ref = s32[2,4,2]{2,1,0:T(4,128)} copy(s32[2,4,2]{1,2,0:T(2,128)} %param.15) | data formatting | bytes 128 | tf_op args[5]
  1.5 1.3 %copy.18.frac_ref = bf16[2,4,3,128]{3,2,1,0:T(4,128)(2,1)} copy(bf16[2,4,3,128]{3,1,2,0:T(4,128)(2,1)} %param.12) | data formatting | bytes 12288 | tf_op args[2]
  2.8 1.9 %message.1.msg_ref = bf16[2,4,56,128]{3,2,1,0:T(8,128)(2,1)} custom-call(bf16[2,4,32,128]{3,2,1,0:T(8,128)(2,1)} %samples_ref.1, bf16[2,4,128]{2,1,0:T(4,128)(2,1)} %density_ref.1, bf16[2,4,3,128]{3,2,1,0:T(4,128)(2,1)} %copy.18.frac_ref, s32[2,4,128]{2,1,0:T(4,128)} %shift_ref.1, s32[2,4,128]{2,1,0:T(4,128)} %depth_ref.1, s32[2,4,2]{2,1,0:T(4,128)} %copy.19.base_ref), custom_call_target="tpu_custom_call" | custom-call | tf_op jit(solution)/shard_map/message/pallas_call | solution.py:92
  4.6 23.1 %gather.1.msg_ref = bf16[32,2,4,56,128]{4,3,2,1,0:T(8,128)(2,1)} custom-call(bf16[2,4,56,128]{3,2,1,0:T(8,128)(2,1)} %message.1.msg_ref), custom_call_target="tpu_custom_call" | custom-call | tf_op jit(solution)/shard_map/gather/pallas_call | solution.py:194
  27.7 1.3 %slice_convert_fusion = s32[32,2,4,1,1]{4,3,2,1,0:T(1,128)S(1)} fusion(bf16[32,2,4,56,128]{4,3,2,1,0:T(8,128)(2,1)} %gather.1.msg_ref), kind=kLoop, calls=%fused_computation.11 | loop fusion | flops 256 | bytes 1536 | tf_op jit(solution)/shard_map/reshape | solution.py:340
  29.0 0.1 copy.20
  29.1 0.1 copy.21
  29.2 0.7 reshape.126.xb_ref
  29.9 0.1 broadcast_in_dim.10
  29.9 0.1 fusion.24
  30.1 0.6 fusion.9.tables_ref
  30.7 54.3 %grid.1 = f32[2,2,4,128,128]{4,3,2,1,0:T(8,128)} custom-call(s32[2,128]{1,0:T(2,128)} %reshape.126.xb_ref, bf16[32,2,4,56,128]{4,3,2,1,0:T(8,128)(2,1)} %gather.1.msg_ref, f32[14,8,128]{2,1,0:T(8,128)} %fusion.9.tables_ref, bf16[256,256]{1,0:T(8,128)(2,1)} %constant.55.clone.right_ref, bf16[256,256]{1,0:T(8,128)(2,1)} %constant.56.clone.left_ref, ...), custom_call_target="tpu_custom_call" | custom-call | tf_op jit(solution)/shard_map/grid/pallas_call | solution.py:302
  85.0 1.3 %convert.7 = bf16[2,2,4,128,128]{4,3,2,1,0:T(8,128)(2,1)S(1)} convert(f32[2,2,4,128,128]{4,3,2,1,0:T(8,128)} %grid.1) | non-fusion elementwise | flops 262144 | bytes 1572864 | tf_op jit(solution)/shard_map/convert.4
  86.3 0.0 copy-start
  86.3 5.2 %collective-permute-start.1 = (bf16[1,2,4,128,128]{4,3,2,1,0:T(8,128)(2,1)S(1)}, bf16[1,2,4,128,128]{4,3,2,1,0:T(8,128)(2,1)S(1)}, u32[]{:S(2)}, u32[]{:S(2)}) collective-permute-start(bf16[1,2,4,128,128]{4,3,2,1,0:T(8,128)(2,1)S(1)} %get-tuple-element.5), channel_id=1, source_target_pairs={{0,32},{32,64},{64,96},{96,128},{128,160},{160,192},{192,224},{1,3... | collective-permute-start | bytes 786440 | tf_op jit(solution)/shard_map/ppermute | solution.py:347
  91.5 1.9 %collective-permute-start = (bf16[1,2,4,128,128]{4,3,2,1,0:T(8,128)(2,1)S(1)}, bf16[1,2,4,128,128]{4,3,2,1,0:T(8,128)(2,1)S(1)}, u32[]{:S(2)}, u32[]{:S(2)}) collective-permute-start(bf16[1,2,4,128,128]{4,3,2,1,0:T(8,128)(2,1)S(1)} %get-tuple-element.6), channel_id=1, source_target_pairs={{32,0},{64,32},{96,64},{128,96},{160,128},{192,160},{224,192},{33,... | collective-permute-start | bytes 786440 | tf_op jit(solution)/shard_map/ppermute | solution.py:348
  93.5 4.2 %collective-permute-done.1 = bf16[1,2,4,128,128]{4,3,2,1,0:T(8,128)(2,1)S(1)} collective-permute-done((bf16[1,2,4,128,128]{4,3,2,1,0:T(8,128)(2,1)S(1)}, bf16[1,2,4,128,128]{4,3,2,1,0:T(8,128)(2,1)S(1)}, u32[]{:S(2)}, u32[]{:S(2)}) %collective-permute-start.1) | collective-permute-done | bytes 262176 | tf_op jit(solution)/shard_map/ppermute | solution.py:347
  97.7 5.3 %collective-permute-done = bf16[1,2,4,128,128]{4,3,2,1,0:T(8,128)(2,1)S(1)} collective-permute-done((bf16[1,2,4,128,128]{4,3,2,1,0:T(8,128)(2,1)S(1)}, bf16[1,2,4,128,128]{4,3,2,1,0:T(8,128)(2,1)S(1)}, u32[]{:S(2)}, u32[]{:S(2)}) %collective-permute-start) | collective-permute-done | bytes 262176 | tf_op jit(solution)/shard_map/ppermute | solution.py:348
  103.0 0.0 copy-done
  103.0 0.2 maximum_subtract_fusion
  103.2 0.3 fusion.5
  103.5 0.4 divide_select_fusion
  103.9 1.2 %fusion.1 = f32[2,2,4,128,128]{4,3,2,1,0:T(8,128)} fusion(f32[2,2,4,128,128]{4,3,2,1,0:T(8,128)S(1)} %copy-done, f32[3,2,4,128,128]{4,3,2,1,0:T(8,128)S(1)} %divide_select_fusion), kind=kLoop, calls=%fused_computation.4 | loop fusion | flops 786432 | bytes 4194304 | tf_op jit(solution)/shard_map/sub | solution.py:356
  (6 shorter events, 0.1 us)
Async XLA Ops:
  86.3 16.7 %copy-start = (f32[2,2,4,128,128]{4,3,2,1,0:T(8,128)S(1)}, f32[2,2,4,128,128]{4,3,2,1,0:T(8,128)}, u32[]{:S(2)}) copy-start(f32[2,2,4,128,128]{4,3,2,1,0:T(8,128)} %grid.1) | copy-start | bytes 3145732
  86.3 11.3 %collective-permute-start.1 = (bf16[1,2,4,128,128]{4,3,2,1,0:T(8,128)(2,1)S(1)}, bf16[1,2,4,128,128]{4,3,2,1,0:T(8,128)(2,1)S(1)}, u32[]{:S(2)}, u32[]{:S(2)}) collective-permute-start(bf16[1,2,4,128,128]{4,3,2,1,0:T(8,128)(2,1)S(1)} %get-tuple-element.5), channel_id=1, source_target_pairs={{0,32},{32,64},{64,96},{96,128},{128,160},{160,192},{192,224},{1,3... | collective-permute-start | bytes 786440 | tf_op jit(solution)/shard_map/ppermute | solution.py:347
  91.5 11.5 %collective-permute-start = (bf16[1,2,4,128,128]{4,3,2,1,0:T(8,128)(2,1)S(1)}, bf16[1,2,4,128,128]{4,3,2,1,0:T(8,128)(2,1)S(1)}, u32[]{:S(2)}, u32[]{:S(2)}) collective-permute-start(bf16[1,2,4,128,128]{4,3,2,1,0:T(8,128)(2,1)S(1)} %get-tuple-element.6), channel_id=1, source_target_pairs={{32,0},{64,32},{96,64},{128,96},{160,128},{192,160},{224,192},{33,... | collective-permute-start | bytes 786440 | tf_op jit(solution)/shard_map/ppermute | solution.py:348
where the time goes:
time: 105 us
  Pallas kernels  79.2 us (75%)
  waiting for transfers between devices  9.47 us (9%)
  starting transfers between devices  7.09 us (7%)
  other arithmetic  5.51 us (5%)
  local copies, waits for them, and re-layouts  3.65 us (3%)
    pallas_call x1, Pallas kernels, half_step(): pl.pallas_call(functools.partial(grid_kernel, grid, coils, rows, blocks,...  54.3 us
    pallas_call x1, Pallas kernels, gather_messages(): pl.pallas_call(functools.partial(gather_kernel, side), out_shape=jax.Shap...  23.1 us
    ppermute x1, waiting for transfers between devices, on_device(): high = lax.ppermute(half[:1].astype(jnp.bfloat16), 'frame', backward)  5.29 us
    ppermute x1, starting transfers between devices, on_device(): low = lax.ppermute(half[-1:].astype(jnp.bfloat16), 'frame', forward)  5.17 us
    ppermute x1, waiting for transfers between devices, on_device(): low = lax.ppermute(half[-1:].astype(jnp.bfloat16), 'frame', forward)  4.18 us
    unnamed x4, local copies, waits for them, and re-layouts  2.66 us
  transfers between devices with their start and end apart: 2, of which 2 were waited for; matrix products, arithmetic and copies ran while one was open for 0% of the time, Pallas kernels for 0%

commit v1 on v0

--- a/solution.py
+++ b/solution.py
@@ -59,11 +59,11 @@
             slot = frame * blocks + block
             lines_ref[slot] = samples_ref[frame, block].astype(jnp.float32) * density_ref[frame, block : block + 1].astype(jnp.float32)
             taps = [
-                jnp.where(row < TAPS, kaiser(offset, frac_ref[frame, block, axis : axis + 1].astype(jnp.float32)), 0.0)
+                jnp.where(row < TAPS, kaiser(offset, frac_ref[frame, axis, block : block + 1].astype(jnp.float32)), 0.0)
                 for axis in range(3)
             ]
-            plane = base_ref[frame, block, 0].astype(jnp.float32)
-            first_row = (shift_ref[frame, block : block + 1] + base_ref[frame, block, 1]) & grid_mask
+            plane = base_ref[frame, 0, block].astype(jnp.float32)
+            first_row = (shift_ref[frame, block : block + 1] + base_ref[frame, 1, block]) & grid_mask
             first_cell = depth_ref[frame, block : block + 1]
             group_x = jnp.where(row == ROW_XB - ROW_WX, plane, taps[0])
             group_y = jnp.where(row == ROW_YB - ROW_WY, first_row.astype(jnp.float32), taps[1])
@@ -74,16 +74,12 @@
             out_ref[frame, block, ROW_WY : ROW_WY + 8] = group_y.astype(jnp.bfloat16)
 
 
-def row_tables(image_rows, grid, lanes):
-    angle_of = lambda index: (index % grid).astype(jnp.float32) * (2.0 * math.pi / grid)
-    turn = angle_of(image_rows[:, None] * jnp.arange(lanes)[None, :])
-    step = jnp.broadcast_to(angle_of(jnp.arange(TAPS)[:, None] * image_rows[None, :])[:, :, None], (TAPS, image_rows.shape[0], lanes))
-    angles = jnp.concatenate([turn[None], step], axis=0)
-    cosine, sine = jnp.cos(angles), jnp.sin(angles)
-    rows = lambda upper, lower: jnp.concatenate([upper, lower], axis=1)
-    return jnp.concatenate(
-        [rows(cosine, sine)[:1], rows(sine, cosine)[:1], rows(cosine, cosine)[1:], rows(-sine, sine)[1:]], axis=0
-    )
+def row_tables(rows, grid, lanes):
+    image_rows = np.arange(grid).reshape(grid // rows, rows, 1)
+    angles = (image_rows * np.arange(lanes) % grid) * (2.0 * np.pi / grid)
+    cosine, sine = np.cos(angles), np.sin(angles)
+    pairs = [(cosine, sine), (sine, cosine), (cosine, cosine), (-sine, sine)]
+    return np.stack([np.concatenate(pair, axis=1) for pair in pairs], axis=1).astype(np.float32)
 
 
 def block_messages(kspace_samples, density, sample_frac, row_offsets, depth_base, block_base):
@@ -96,7 +92,7 @@
         out_specs=vmem,
         scratch_shapes=[pltpu.VMEM((frames * blocks, channels, lanes), jnp.float32)],
         name="message",
-    )(kspace_samples, density, sample_frac, row_offsets, depth_base, block_base)
+    )(kspace_samples, density, jnp.swapaxes(sample_frac, 1, 2), row_offsets, depth_base, jnp.swapaxes(block_base, 1, 2))
 
 
 def gather_kernel(side, msg_ref, out_ref, send_sem, recv_sem, own_sem):
@@ -206,17 +202,21 @@
     )(message)
 
 
-def grid_kernel(grid, coils, rows, blocks, scale, xb_ref, msg_ref, tables_ref, right_ref, left_ref, maps_ref, est_ref, out_ref, acc_ref):
-    frame = pl.program_id(0)
+def grid_kernel(grid, coils, rows, blocks, scale, tile_ref, msg_ref, tables_ref, right_ref, left_ref, maps_ref, est_ref, out_ref, acc_ref, steps_ref):
+    here = tile_ref[0]
     half_rows = rows * coils
     plane = 2 * half_rows
     per_tile = msg_ref.shape[2]
+    pitch = plane + 8
 
     def clear(step, carry):
         acc_ref[pl.ds(pl.multiple_of(step * 128, 128), 128), :] = jnp.zeros((128, grid), jnp.float32)
         return carry
 
-    lax.fori_loop(0, grid * plane // 128, clear, 0, unroll=4)
+    lax.fori_loop(0, grid * pitch // 128, clear, 0, unroll=4)
+    for tap in range(TAPS):
+        steps_ref[tap] = jnp.broadcast_to(tables_ref[here, 2][:, tap : tap + 1], (2 * rows, 128))
+        steps_ref[TAPS + tap] = jnp.broadcast_to(tables_ref[here, 3][:, tap : tap + 1], (2 * rows, 128))
     cells = lax.broadcasted_iota(jnp.int32, (8, 128), 0)
 
     def one_block(block, carry):
@@ -228,29 +228,37 @@
         tail = msg_ref[tile, 0, local, ROW_WY : ROW_WY + 8, :].astype(jnp.float32)
         first_row = jnp.broadcast_to(tail[ROW_YB - ROW_WY : ROW_YB - ROW_WY + 1, :].astype(jnp.int32), (8, 128))
         first_cell = tail[ROW_ZB - ROW_WY : ROW_ZB - ROW_WY + 1, :].astype(jnp.int32)
-        turn = jnp.take_along_axis(tables_ref[0], first_row, axis=1)
-        swapped = jnp.take_along_axis(tables_ref[1], first_row, axis=1)
-        sum_same = sum(tail[e : e + 1] * tables_ref[2 + e] for e in range(TAPS))
-        sum_cross = sum(tail[e : e + 1] * tables_ref[2 + TAPS + e] for e in range(TAPS))
+        turn = jnp.take_along_axis(tables_ref[here, 0], first_row, axis=1)
+        swapped = jnp.take_along_axis(tables_ref[here, 1], first_row, axis=1)
+        sum_same = sum(tail[e : e + 1] * steps_ref[e] for e in range(TAPS))
+        sum_cross = sum(tail[e : e + 1] * steps_ref[TAPS + e] for e in range(TAPS))
         phase = turn * sum_same + swapped * sum_cross
         reals = [real * phase[y : y + 1] - imag * phase[rows + y : rows + y + 1] for y in range(rows)]
         imags = [real * phase[rows + y : rows + y + 1] + imag * phase[y : y + 1] for y in range(rows)]
         field = jnp.concatenate(reals + imags, axis=0)
-        lag0 = cells - first_cell
-        pieces = []
-        for group in range(grid // 8):
-            lag = jnp.minimum((lag0 + group * 8) & (grid - 1), 7)
-            pieces.append(jnp.take_along_axis(depth, lag, axis=0))
-        spread = jnp.concatenate(pieces, axis=0).astype(jnp.bfloat16)
-        left = jnp.concatenate([(field * weights[tap : tap + 1]).astype(jnp.bfloat16) for tap in range(TAPS)], axis=0)
+        low = cells - (first_cell & 15)
+        inside = [jnp.take_along_axis(depth, jnp.minimum((low + part) & 31, 7), axis=0) for part in (0, 8)]
+        after = [jnp.take_along_axis(depth, jnp.minimum(low + part, 7), axis=0) for part in (16, 24)]
+        inside = jnp.concatenate(inside, axis=0).astype(jnp.bfloat16)
+        after = jnp.concatenate(after, axis=0).astype(jnp.bfloat16)
+        group = jnp.broadcast_to((first_cell >> 4).astype(jnp.float32), (16, 128)).astype(jnp.bfloat16)
+        hits = [group == jnp.asarray(index, jnp.bfloat16) for index in range(grid // 16)]
+        nothing = jnp.zeros((16, 128), jnp.bfloat16)
+        spread = jnp.concatenate(
+            [jnp.where(hits[index], inside, jnp.where(hits[index - 1], after, nothing)) for index in range(grid // 16)], axis=0
+        )
+        field16 = field.astype(jnp.bfloat16).reshape(plane // 16, 16, 128)
+        left = jnp.concatenate(
+            [field16 * jnp.broadcast_to(weights[tap : tap + 1], (16, 128)).astype(jnp.bfloat16)[None] for tap in range(TAPS)], axis=0
+        ).reshape(TAPS * plane, 128)
         value = lax.dot_general(left, spread, (((1,), (1,)), ((), ())), preferred_element_type=jnp.float32)
-        first_plane = xb_ref[frame, block]
+        first_plane = weights[ROW_XB - ROW_WX : ROW_XB - ROW_WX + 1, :].astype(jnp.int32)[0, 0]
         for tap in range(TAPS):
-            start = pl.multiple_of(((first_plane + tap) & (grid - 1)) * plane, plane)
+            start = pl.multiple_of(((first_plane + tap) & (grid - 1)) * pitch, 8)
             acc_ref[pl.ds(start, plane), :] += value[tap * plane : (tap + 1) * plane]
         return carry
 
-    lax.fori_loop(0, blocks, one_block, 0, unroll=4)
+    lax.fori_loop(0, blocks, one_block, 0, unroll=32)
 
     right = right_ref[...]
     left = left_ref[...]
@@ -263,8 +271,8 @@
             lines = []
             for part in range(2):
                 base = y * coils + coil + part
-                re = acc_ref[pl.ds(base, grid, stride=plane), :]
-                im = acc_ref[pl.ds(half_rows + base, grid, stride=plane), :]
+                re = acc_ref[pl.ds(base, grid, stride=pitch), :]
+                im = acc_ref[pl.ds(half_rows + base, grid, stride=pitch), :]
                 lines.append(jnp.concatenate([re, im], axis=1).astype(jnp.bfloat16))
             second = jnp.dot(jnp.concatenate(lines, axis=0), right, preferred_element_type=jnp.float32).astype(jnp.bfloat16)
             stacked = jnp.concatenate(
@@ -293,11 +301,12 @@
         out_ref[0, 1, y] = est_ref[0, 1, y] + scale * out_ref[0, 1, y]
 
 
-def half_step(gathered, first_plane, tables, coil_maps, estimate, scale):
+def half_step(gathered, tile, coil_maps, estimate, scale):
     tiles, frames, per_tile = gathered.shape[:3]
     coils, _, rows, grid, _ = coil_maps.shape
     blocks = tiles * per_tile
     right, left = (jnp.asarray(table, jnp.bfloat16) for table in dft_tables(grid))
+    tables = jnp.asarray(row_tables(rows, grid, gathered.shape[-1]))
     once = pl.Buffered(1)
     return pl.pallas_call(
         functools.partial(grid_kernel, grid, coils, rows, blocks, scale),
@@ -307,18 +316,21 @@
             grid=(frames,),
             in_specs=[
                 pl.BlockSpec((tiles, 1, per_tile, ROWS, 128), lambda f, s: (0, f, 0, 0, 0)),
-                pl.BlockSpec(tables.shape, lambda f, s: (0, 0, 0), pipeline_mode=once),
+                pl.BlockSpec(tables.shape, lambda f, s: (0, 0, 0, 0), pipeline_mode=once),
                 pl.BlockSpec((2 * grid, 2 * grid), lambda f, s: (0, 0), pipeline_mode=once),
                 pl.BlockSpec((2 * grid, 2 * grid), lambda f, s: (0, 0), pipeline_mode=once),
                 pl.BlockSpec(coil_maps.shape, lambda f, s: (0, 0, 0, 0, 0), pipeline_mode=once),
                 pl.BlockSpec((1, 2, rows, grid, grid), lambda f, s: (f, 0, 0, 0, 0)),
             ],
             out_specs=pl.BlockSpec((1, 2, rows, grid, grid), lambda f, s: (f, 0, 0, 0, 0)),
-            scratch_shapes=[pltpu.VMEM((grid * 2 * rows * coils, grid), jnp.float32)],
+            scratch_shapes=[
+                pltpu.VMEM((grid * (2 * rows * coils + 8), grid), jnp.float32),
+                pltpu.VMEM((2 * TAPS, 2 * rows, 128), jnp.float32),
+            ],
         ),
         compiler_params=pltpu.CompilerParams(vmem_limit_bytes=56 * 1024 * 1024),
         name="grid",
-    )(first_plane, gathered, tables, right, left, coil_maps, estimate)
+    )(tile, gathered, tables, right, left, coil_maps, estimate)
 
 
 def on_device(
@@ -336,10 +348,7 @@
     message = block_messages(kspace_samples, density, sample_frac, row_offsets, depth_base, block_base)
     gathered = gather_messages(message, tile_count, math.isqrt(tile_count // 2))
 
-    first_plane = gathered[:, :, :, ROW_XB, 0].astype(jnp.int32)
-    first_plane = jnp.moveaxis(first_plane, 1, 0).reshape(frames, tile_count * per_tile)
-    tables = row_tables(tile_here * rows + jnp.arange(rows), grid, samples)
-    half = half_step(gathered, first_plane, tables, coil_maps, estimate, scale)
+    half = half_step(gathered, tile_here.reshape(1), coil_maps, estimate, scale)
 
     count = lax.axis_size("frame")
     forward = [(i, i + 1) for i in range(count - 1)]

time: 105 us -> 79.8 us (0.76)
  Pallas kernels: 79.2 us -> 59.5 us
  local copies, waits for them, and re-layouts: 3.65 us -> 0.04 us
  other arithmetic: 5.51 us -> 3.4 us
    pallas_call x1, Pallas kernels: 54.3 us -> 34.6 us  [half_step(): pl.pallas_call(functools.partial(grid_kernel, grid, coils, rows, blocks,...]
    unnamed x4 -> x2, local copies, waits for them, and re-layouts: 2.66 us -> 0.01 us
    reshape x1 -> x0, other arithmetic: 1.27 us -> none  [on_device(): jnp.moveaxis(first_plane, 1, 0).reshape(frames, tile_count * per_tile)]
where the time goes in v1:
time: 79.8 us; the launch traced here: 79.6 us
  Pallas kernels  59.5 us (75%)
  waiting for transfers between devices  9.47 us (12%)
  starting transfers between devices  7.09 us (9%)
  other arithmetic  3.4 us (4%)
    pallas_call x1, Pallas kernels, half_step(): pl.pallas_call(functools.partial(grid_kernel, grid, coils, rows, blocks,...  34.6 us
    pallas_call x1, Pallas kernels, gather_messages(): pl.pallas_call(functools.partial(gather_kernel, side), out_shape=jax.Shap...  23.1 us
    ppermute x1, waiting for transfers between devices, on_device(): high = lax.ppermute(half[:1].astype(jnp.bfloat16), 'frame', backward)  5.29 us
    ppermute x1, starting transfers between devices, on_device(): low = lax.ppermute(half[-1:].astype(jnp.bfloat16), 'frame', forward)  5.17 us
    ppermute x1, waiting for transfers between devices, on_device(): low = lax.ppermute(half[-1:].astype(jnp.bfloat16), 'frame', forward)  4.18 us
    ppermute x1, starting transfers between devices, on_device(): high = lax.ppermute(half[:1].astype(jnp.bfloat16), 'frame', backward)  1.92 us
    pallas_call x1, Pallas kernels, block_messages(): pl.pallas_call(message_kernel, out_shape=jax.ShapeDtypeStruct((frames, bl...  1.86 us
  transfers between devices with their start and end apart: 2, of which 2 were waited for; matrix products, arithmetic and copies ran while one was open for 0% of the time, Pallas kernels for 0%

profile of v1, /device:TPU:96, one launch (start us, length us, event | category | flops | bytes accessed | tf_op | source)
XLA Modules:
  0.0 79.6 jit_solution(551065809927345914)
XLA Ops:
  0.0 1.9 %message.1.msg_ref = bf16[2,4,56,128]{3,2,1,0:T(8,128)(2,1)} custom-call(bf16[2,4,32,128]{3,2,1,0:T(8,128)(2,1)} %samples_ref.1, bf16[2,4,128]{2,1,0:T(4,128)(2,1)} %density_ref.1, bf16[2,3,4,128]{3,2,1,0:T(4,128)(2,1)} %bitcast.5, s32[2,4,128]{2,1,0:T(4,128)} %shift_ref.1, s32[2,4,128]{2,1,0:T(4,128)} %depth_ref.1, s32[2,2,4]{2,1,0:T(2,128)} %bitcast.6), custom_call_target="tpu_custom_call" | custom-call | tf_op jit(solution)/shard_map/message/pallas_call | solution.py:88
  1.9 23.1 %gather.1.msg_ref = bf16[32,2,4,56,128]{4,3,2,1,0:T(8,128)(2,1)} custom-call(bf16[2,4,56,128]{3,2,1,0:T(8,128)(2,1)} %message.1.msg_ref), custom_call_target="tpu_custom_call" | custom-call | tf_op jit(solution)/shard_map/gather/pallas_call | solution.py:190
  25.0 34.6 %grid.1 = f32[2,2,4,128,128]{4,3,2,1,0:T(8,128)} custom-call(s32[1]{0:T(128)} %bitcast.tile_ref, bf16[32,2,4,56,128]{4,3,2,1,0:T(8,128)(2,1)} %gather.1.msg_ref, f32[32,4,8,128]{3,2,1,0:T(8,128)} %constant.32.clone.tables_ref, bf16[256,256]{1,0:T(8,128)(2,1)} %constant.30.clone.right_ref, bf16[256,256]{1,0:T(8,128)(2,1)} %constant.31.clone.left_ref, ...), custom_call_target="tpu_custom_call" | custom-call | tf_op jit(solution)/shard_map/grid/pallas_call | solution.py:311
  59.5 1.3 %convert.4 = bf16[2,2,4,128,128]{4,3,2,1,0:T(8,128)(2,1)S(1)} convert(f32[2,2,4,128,128]{4,3,2,1,0:T(8,128)} %grid.1) | non-fusion elementwise | flops 262144 | bytes 1572864 | tf_op jit(solution)/shard_map/convert.1
  60.8 0.0 copy-start
  60.9 5.2 %collective-permute-start.1 = (bf16[1,2,4,128,128]{4,3,2,1,0:T(8,128)(2,1)S(1)}, bf16[1,2,4,128,128]{4,3,2,1,0:T(8,128)(2,1)S(1)}, u32[]{:S(2)}, u32[]{:S(2)}) collective-permute-start(bf16[1,2,4,128,128]{4,3,2,1,0:T(8,128)(2,1)S(1)} %get-tuple-element.5), channel_id=1, source_target_pairs={{0,32},{32,64},{64,96},{96,128},{128,160},{160,192},{192,224},{1,3... | collective-permute-start | bytes 786440 | tf_op jit(solution)/shard_map/ppermute | solution.py:356
  66.1 1.9 %collective-permute-start = (bf16[1,2,4,128,128]{4,3,2,1,0:T(8,128)(2,1)S(1)}, bf16[1,2,4,128,128]{4,3,2,1,0:T(8,128)(2,1)S(1)}, u32[]{:S(2)}, u32[]{:S(2)}) collective-permute-start(bf16[1,2,4,128,128]{4,3,2,1,0:T(8,128)(2,1)S(1)} %get-tuple-element.6), channel_id=1, source_target_pairs={{32,0},{64,32},{96,64},{128,96},{160,128},{192,160},{224,192},{33,... | collective-permute-start | bytes 786440 | tf_op jit(solution)/shard_map/ppermute | solution.py:357
  68.0 4.2 %collective-permute-done.1 = bf16[1,2,4,128,128]{4,3,2,1,0:T(8,128)(2,1)S(1)} collective-permute-done((bf16[1,2,4,128,128]{4,3,2,1,0:T(8,128)(2,1)S(1)}, bf16[1,2,4,128,128]{4,3,2,1,0:T(8,128)(2,1)S(1)}, u32[]{:S(2)}, u32[]{:S(2)}) %collective-permute-start.1) | collective-permute-done | bytes 262176 | tf_op jit(solution)/shard_map/ppermute | solution.py:356
  72.2 5.3 %collective-permute-done = bf16[1,2,4,128,128]{4,3,2,1,0:T(8,128)(2,1)S(1)} collective-permute-done((bf16[1,2,4,128,128]{4,3,2,1,0:T(8,128)(2,1)S(1)}, bf16[1,2,4,128,128]{4,3,2,1,0:T(8,128)(2,1)S(1)}, u32[]{:S(2)}, u32[]{:S(2)}) %collective-permute-start) | collective-permute-done | bytes 262176 | tf_op jit(solution)/shard_map/ppermute | solution.py:357
  77.6 0.0 copy-done
  77.6 0.2 maximum_subtract_fusion
  77.7 0.3 fusion.5
  78.0 0.4 divide_select_fusion
  78.4 1.2 %fusion.1 = f32[2,2,4,128,128]{4,3,2,1,0:T(8,128)} fusion(f32[2,2,4,128,128]{4,3,2,1,0:T(8,128)S(1)} %copy-done, f32[3,2,4,128,128]{4,3,2,1,0:T(8,128)S(1)} %divide_select_fusion), kind=kLoop, calls=%fused_computation.4 | loop fusion | flops 786432 | bytes 4194304 | tf_op jit(solution)/shard_map/sub | solution.py:365
  (4 shorter events, 0.1 us)
Async XLA Ops:
  60.8 16.7 %copy-start = (f32[2,2,4,128,128]{4,3,2,1,0:T(8,128)S(1)}, f32[2,2,4,128,128]{4,3,2,1,0:T(8,128)}, u32[]{:S(2)}) copy-start(f32[2,2,4,128,128]{4,3,2,1,0:T(8,128)} %grid.1) | copy-start | bytes 3145732
  60.9 11.3 %collective-permute-start.1 = (bf16[1,2,4,128,128]{4,3,2,1,0:T(8,128)(2,1)S(1)}, bf16[1,2,4,128,128]{4,3,2,1,0:T(8,128)(2,1)S(1)}, u32[]{:S(2)}, u32[]{:S(2)}) collective-permute-start(bf16[1,2,4,128,128]{4,3,2,1,0:T(8,128)(2,1)S(1)} %get-tuple-element.5), channel_id=1, source_target_pairs={{0,32},{32,64},{64,96},{96,128},{128,160},{160,192},{192,224},{1,3... | collective-permute-start | bytes 786440 | tf_op jit(solution)/shard_map/ppermute | solution.py:356
  66.1 11.5 %collective-permute-start = (bf16[1,2,4,128,128]{4,3,2,1,0:T(8,128)(2,1)S(1)}, bf16[1,2,4,128,128]{4,3,2,1,0:T(8,128)(2,1)S(1)}, u32[]{:S(2)}, u32[]{:S(2)}) collective-permute-start(bf16[1,2,4,128,128]{4,3,2,1,0:T(8,128)(2,1)S(1)} %get-tuple-element.6), channel_id=1, source_target_pairs={{32,0},{64,32},{96,64},{128,96},{160,128},{192,160},{224,192},{33,... | collective-permute-start | bytes 786440 | tf_op jit(solution)/shard_map/ppermute | solution.py:357

commit v2 on v1

--- a/solution.py
+++ b/solution.py
@@ -115,74 +115,108 @@
         pl.semaphore_signal(barrier, inc=1, device_id={"tile": device}, device_id_type=MESH)
     pl.semaphore_wait(barrier, len(neighbours))
 
-    def whole(number, slot, target, own=False):
-        return pltpu.make_async_remote_copy(
-            src_ref=msg_ref if own else out_ref.at[slot],
-            dst_ref=out_ref.at[slot],
+    copies = {}
+
+    def make(key, slot, frame, target, own):
+        number = len(copies)
+        source = msg_ref if own else out_ref.at[slot]
+        copies[key] = pltpu.make_async_remote_copy(
+            src_ref=source if frame is None else source.at[frame],
+            dst_ref=out_ref.at[slot] if frame is None else out_ref.at[slot, frame],
             send_sem=send_sem.at[number],
             recv_sem=recv_sem.at[number],
             device_id={"tile": target},
             device_id_type=MESH,
         )
 
-    def part(number, slot, frame, target):
-        return pltpu.make_async_remote_copy(
-            src_ref=out_ref.at[slot, frame],
-            dst_ref=out_ref.at[slot, frame],
-            send_sem=send_sem.at[number],
-            recv_sem=recv_sem.at[number],
-            device_id={"tile": target},
-            device_id_type=MESH,
-        )
-
-    copies = {0: whole(0, tile, at(1, 0), True), 1: whole(1, tile, at(-1, 0), True)}
-    copies[2] = part(2, at(-1, 0), 0, at(1, 0))
-    copies[3] = part(3, at(1, 0), 1, at(-1, 0))
-    places = [0, -1, 1, 2]
-    for index, along in enumerate(places):
-        base = 4 + 4 * index
-        copies[base] = whole(base, at(along, 0), at(0, 1), along == 0)
-        copies[base + 1] = whole(base + 1, at(along, 0), at(0, -1), along == 0)
-        copies[base + 2] = part(base + 2, at(along, -1), 0, at(0, 1))
-        copies[base + 3] = part(base + 3, at(along, 1), 1, at(0, -1))
-        for turn, across in enumerate(places):
-            number = 20 + 4 * index + turn
-            copies[number] = whole(number, at(along, across), partner, along == 0 and across == 0)
-
-    def start(*numbers):
-        for number in numbers:
-            copies[number].start()
-
-    def arrived(*numbers):
-        for number in numbers:
-            copies[number].wait_recv()
+    for frame in (0, 1):
+        for way in (1, -1):
+            make(("first", 0, frame, way), tile, frame, at(way, 0), True)
+    make(("pass", 0), at(-1, 0), 0, at(1, 0), False)
+    make(("pass", 1), at(1, 0), 1, at(-1, 0), False)
+    for along in (0, -1, 1, 2):
+        for frame in (0, 1):
+            for way in (1, -1):
+                make(("second", along, frame, way), at(along, 0), frame, at(0, way), along == 0)
+        make(("hand", along, 0), at(along, -1), 0, at(0, 1), False)
+        make(("hand", along, 1), at(along, 1), 1, at(0, -1), False)
+        for across in (0, -1, 1, 2):
+            make(("core", along, across), at(along, across), None, partner, along == 0 and across == 0)
+
+    def start(*keys):
+        for key in keys:
+            copies[key].start()
+
+    def arrived(*keys):
+        for key in keys:
+            copies[key].wait_recv()
+
+    def second(along, *frames):
+        for frame in frames:
+            way = 1 - 2 * frame
+            start(("second", along, frame, way), ("second", along, frame, -way))
+
+    there = {}
+
+    def to_core(along, across, *frames):
+        there[along, across] = there.get((along, across), 0) + len(frames)
+        if there[along, across] == 2:
+            start(("core", along, across))
 
     own = pltpu.make_async_copy(msg_ref, out_ref.at[tile], own_sem)
-    start(0, 1, 4, 5, 20)
+    start(("first", 0, 0, 1), ("first", 0, 1, -1), ("first", 0, 1, 1), ("first", 0, 0, -1))
+    second(0, 0, 1)
     own.start()
-    arrived(0)
-    start(2, 8, 9, 24)
-    arrived(1)
-    start(3, 12, 13, 28)
-    arrived(4)
-    start(6, 21)
-    arrived(5)
-    start(7, 22)
-    arrived(2, 3)
-    start(16, 17, 32)
-    for index in (1, 2, 3):
-        base = 4 + 4 * index
-        arrived(base)
-        start(base + 2, 20 + 4 * index + 1)
-        arrived(base + 1)
-        start(base + 3, 20 + 4 * index + 2)
-    for index in range(4):
-        base = 4 + 4 * index
-        arrived(base + 2, base + 3)
-        start(20 + 4 * index + 3)
-    arrived(*range(20, 36))
-    for number in range(36):
-        copies[number].wait_send()
+    to_core(0, 0, 0, 1)
+    arrived(("first", 0, 0, 1))
+    start(("pass", 0))
+    second(-1, 0)
+    to_core(-1, 0, 0)
+    arrived(("first", 0, 1, -1))
+    start(("pass", 1))
+    second(1, 1)
+    to_core(1, 0, 1)
+    arrived(("first", 0, 1, 1))
+    second(-1, 1)
+    to_core(-1, 0, 1)
+    arrived(("first", 0, 0, -1))
+    second(1, 0)
+    to_core(1, 0, 0)
+    arrived(("second", 0, 0, 1))
+    start(("hand", 0, 0))
+    to_core(0, -1, 0)
+    arrived(("second", 0, 1, -1))
+    start(("hand", 0, 1))
+    to_core(0, 1, 1)
+    arrived(("pass", 0))
+    second(2, 0)
+    to_core(2, 0, 0)
+    arrived(("pass", 1))
+    second(2, 1)
+    to_core(2, 0, 1)
+    arrived(("second", 0, 1, 1))
+    to_core(0, -1, 1)
+    arrived(("second", 0, 0, -1))
+    to_core(0, 1, 0)
+    for along in (-1, 1, 2):
+        order = (0, 1) if along != 1 else (1, 0)
+        for frame in order:
+            way = 1 - 2 * frame
+            arrived(("second", along, frame, way))
+            start(("hand", along, frame))
+            to_core(along, -way, frame)
+        for frame in order:
+            way = 1 - 2 * frame
+            arrived(("second", along, frame, -way))
+            to_core(along, way, frame)
+    for along in (0, -1, 1, 2):
+        for frame in (0, 1):
+            arrived(("hand", along, frame))
+            to_core(along, 2, frame)
+    for key in [key for key in copies if key[0] == "core"]:
+        copies[key].wait_recv()
+    for copy in copies.values():
+        copy.wait_send()
     own.wait()
 
 
@@ -193,8 +227,8 @@
         in_specs=[pl.BlockSpec(memory_space=pltpu.VMEM)],
         out_specs=pl.BlockSpec(memory_space=pl.ANY),
         scratch_shapes=[
-            pltpu.SemaphoreType.DMA((36,)),
-            pltpu.SemaphoreType.DMA((36,)),
+            pltpu.SemaphoreType.DMA((46,)),
+            pltpu.SemaphoreType.DMA((46,)),
             pltpu.SemaphoreType.DMA(()),
         ],
         compiler_params=pltpu.CompilerParams(collective_id=0, has_side_effects=True),
@@ -202,7 +236,7 @@
     )(message)
 
 
-def grid_kernel(grid, coils, rows, blocks, scale, tile_ref, msg_ref, tables_ref, right_ref, left_ref, maps_ref, est_ref, out_ref, acc_ref, steps_ref):
+def grid_kernel(grid, coils, rows, blocks, scale, tile_ref, msg_ref, tables_ref, right_ref, left_ref, maps_ref, est_ref, out_ref, sent_ref, acc_ref, steps_ref):
     here = tile_ref[0]
     half_rows = rows * coils
     plane = 2 * half_rows
@@ -297,8 +331,10 @@
             return carry
 
         lax.fori_loop(0, coils // 2, one_pair, 0, unroll=8)
-        out_ref[0, 0, y] = est_ref[0, 0, y] + scale * out_ref[0, 0, y]
-        out_ref[0, 1, y] = est_ref[0, 1, y] + scale * out_ref[0, 1, y]
+        for part in range(2):
+            half = est_ref[0, part, y] + scale * out_ref[0, part, y]
+            out_ref[0, part, y] = half
+            sent_ref[0, part, y] = half.astype(jnp.bfloat16)
 
 
 def half_step(gathered, tile, coil_maps, estimate, scale):
@@ -310,7 +346,7 @@
     once = pl.Buffered(1)
     return pl.pallas_call(
         functools.partial(grid_kernel, grid, coils, rows, blocks, scale),
-        out_shape=jax.ShapeDtypeStruct(estimate.shape, jnp.float32),
+        out_shape=[jax.ShapeDtypeStruct(estimate.shape, kind) for kind in (jnp.float32, jnp.bfloat16)],
         grid_spec=pltpu.PrefetchScalarGridSpec(
             num_scalar_prefetch=1,
             grid=(frames,),
@@ -322,7 +358,7 @@
                 pl.BlockSpec(coil_maps.shape, lambda f, s: (0, 0, 0, 0, 0), pipeline_mode=once),
                 pl.BlockSpec((1, 2, rows, grid, grid), lambda f, s: (f, 0, 0, 0, 0)),
             ],
-            out_specs=pl.BlockSpec((1, 2, rows, grid, grid), lambda f, s: (f, 0, 0, 0, 0)),
+            out_specs=[pl.BlockSpec((1, 2, rows, grid, grid), lambda f, s: (f, 0, 0, 0, 0))] * 2,
             scratch_shapes=[
                 pltpu.VMEM((grid * (2 * rows * coils + 8), grid), jnp.float32),
                 pltpu.VMEM((2 * TAPS, 2 * rows, 128), jnp.float32),
@@ -331,6 +367,80 @@
         compiler_params=pltpu.CompilerParams(vmem_limit_bytes=56 * 1024 * 1024),
         name="grid",
     )(tile, gathered, tables, right, left, coil_maps, estimate)
+
+
+def exchange_kernel(count, half_ref, before_ref, after_ref, send_sem, recv_sem):
+    here = lax.axis_index("frame")
+    upper, lower = (here + 1) % count, (here + count - 1) % count
+    barrier = pltpu.get_barrier_semaphore()
+    for device in (upper, lower):
+        pl.semaphore_signal(barrier, inc=1, device_id={"frame": device}, device_id_type=MESH)
+    pl.semaphore_wait(barrier, 2)
+    copies = [
+        pltpu.make_async_remote_copy(
+            src_ref=half_ref.at[frame],
+            dst_ref=target,
+            send_sem=send_sem.at[number],
+            recv_sem=recv_sem.at[number],
+            device_id={"frame": device},
+            device_id_type=MESH,
+        )
+        for number, (frame, target, device) in enumerate(
+            [(half_ref.shape[0] - 1, before_ref, upper), (0, after_ref, lower)]
+        )
+    ]
+    for copy in copies:
+        copy.start()
+    for copy in copies:
+        copy.wait()
+
+
+def exchange_frames(half, count):
+    anywhere = pl.BlockSpec(memory_space=pl.ANY)
+    return pl.pallas_call(
+        functools.partial(exchange_kernel, count),
+        out_shape=[jax.ShapeDtypeStruct(half.shape[1:], half.dtype)] * 2,
+        in_specs=[anywhere],
+        out_specs=[anywhere] * 2,
+        scratch_shapes=[pltpu.SemaphoreType.DMA((2,)), pltpu.SemaphoreType.DMA((2,))],
+        compiler_params=pltpu.CompilerParams(collective_id=1, has_side_effects=True),
+        name="exchange",
+    )(half)
+
+
+def variation_kernel(count, frame_ref, half_ref, before_ref, after_ref, out_ref):
+    here = frame_ref[0]
+
+    def psi(later, earlier):
+        change = [later[part] - earlier[part] for part in range(2)]
+        factor = lax.rsqrt(change[0] * change[0] + change[1] * change[1] + EPS * EPS)
+        return [change[part] * factor for part in range(2)]
+
+    first = [half_ref[0, part, 0] for part in range(2)]
+    last = [half_ref[1, part, 0] for part in range(2)]
+    before = [before_ref[part, 0].astype(jnp.float32) for part in range(2)]
+    after = [after_ref[part, 0].astype(jnp.float32) for part in range(2)]
+    psi_before, psi_here, psi_after = psi(first, before), psi(last, first), psi(after, last)
+    for part in range(2):
+        low = jnp.where(here > 0, psi_before[part], 0.0)
+        high = jnp.where(here < count - 1, psi_after[part], 0.0)
+        out_ref[0, part, 0] = first[part] - LAMBDA_TV * (low - psi_here[part])
+        out_ref[1, part, 0] = last[part] - LAMBDA_TV * (psi_here[part] - high)
+
+
+def variation_step(half, before, after, frame_here, count):
+    frames, parts, rows, grid, _ = half.shape
+    assert frames == 2
+    whole = pl.BlockSpec((frames, parts, 1, grid, grid), lambda y, s: (0, 0, y, 0, 0))
+    side = pl.BlockSpec((parts, 1, grid, grid), lambda y, s: (0, y, 0, 0))
+    return pl.pallas_call(
+        functools.partial(variation_kernel, count),
+        out_shape=jax.ShapeDtypeStruct(half.shape, half.dtype),
+        grid_spec=pltpu.PrefetchScalarGridSpec(
+            num_scalar_prefetch=1, grid=(rows,), in_specs=[whole, side, side], out_specs=whole
+        ),
+        name="variation",
+    )(frame_here, half, before, after)
 
 
 def on_device(
@@ -348,21 +458,9 @@
     message = block_messages(kspace_samples, density, sample_frac, row_offsets, depth_base, block_base)
     gathered = gather_messages(message, tile_count, math.isqrt(tile_count // 2))
 
-    half = half_step(gathered, tile_here.reshape(1), coil_maps, estimate, scale)
-
-    count = lax.axis_size("frame")
-    forward = [(i, i + 1) for i in range(count - 1)]
-    backward = [(target, source) for source, target in forward]
-    low = lax.ppermute(half[-1:].astype(jnp.bfloat16), "frame", forward)
-    high = lax.ppermute(half[:1].astype(jnp.bfloat16), "frame", backward)
-    padded = jnp.concatenate([low.astype(jnp.float32), half, high.astype(jnp.float32)], axis=0)
-    change = padded[1:] - padded[:-1]
-    magnitude = jnp.sqrt(change[:, 0] * change[:, 0] + change[:, 1] * change[:, 1] + EPS * EPS)
-    psi = change / magnitude[:, None]
-    pair_index = frame_here * frames + jnp.arange(frames + 1) - 1
-    valid = (pair_index >= 0) & (pair_index <= count * frames - 2)
-    psi = jnp.where(valid[:, None, None, None, None], psi, 0.0)
-    return half - LAMBDA_TV * (psi[:-1] - psi[1:])
+    half, rounded = half_step(gathered, tile_here.reshape(1), coil_maps, estimate, scale)
+    before, after = exchange_frames(rounded, lax.axis_size("frame"))
+    return variation_step(half, before, after, frame_here.reshape(1), lax.axis_size("frame"))
 
 
 def solution(mesh):

time: 79.8 us -> 76.7 us (0.961)
  the two profiles are of different devices: /device:TPU:96 before, /device:TPU:1 now
where the time goes in v2:
time: 76.7 us; the launch traced here: 76.5 us
  Pallas kernels  76.5 us (100%)
    pallas_call x1, Pallas kernels, half_step(): pl.pallas_call(functools.partial(grid_kernel, grid, coils, rows, blocks,...  34.6 us
    pallas_call x1, Pallas kernels, gather_messages(): pl.pallas_call(functools.partial(gather_kernel, side), out_shape=jax.Shap...  23.5 us
    pallas_call x1, Pallas kernels, exchange_frames(): pl.pallas_call(functools.partial(exchange_kernel, count), out_shape=[jax....  13 us
    pallas_call x1, Pallas kernels, variation_step(): pl.pallas_call(functools.partial(variation_kernel, count), out_shape=jax....  3.57 us
    pallas_call x1, Pallas kernels, block_messages(): pl.pallas_call(message_kernel, out_shape=jax.ShapeDtypeStruct((frames, bl...  1.86 us

profile of v2, /device:TPU:1, one launch (start us, length us, event | category | flops | bytes accessed | tf_op | source)
XLA Modules:
  0.0 76.5 jit_solution(2446860951859367285)
XLA Ops:
  0.0 1.9 %message.1.msg_ref = bf16[2,4,56,128]{3,2,1,0:T(8,128)(2,1)} custom-call(bf16[2,4,32,128]{3,2,1,0:T(8,128)(2,1)} %samples_ref.1, bf16[2,4,128]{2,1,0:T(4,128)(2,1)} %density_ref.1, bf16[2,3,4,128]{3,2,1,0:T(4,128)(2,1)} %bitcast.4, s32[2,4,128]{2,1,0:T(4,128)} %shift_ref.1, s32[2,4,128]{2,1,0:T(4,128)} %depth_ref.1, s32[2,2,4]{2,1,0:T(2,128)} %bitcast.5), custom_call_target="tpu_custom_call" | custom-call | tf_op jit(solution)/shard_map/message/pallas_call | solution.py:88
  1.9 23.5 %gather.1.msg_ref = bf16[32,2,4,56,128]{4,3,2,1,0:T(8,128)(2,1)} custom-call(bf16[2,4,56,128]{3,2,1,0:T(8,128)(2,1)} %message.1.msg_ref), custom_call_target="tpu_custom_call" | custom-call | tf_op jit(solution)/shard_map/gather/pallas_call | solution.py:224
  25.4 34.6 %grid.1 = (f32[2,2,4,128,128]{4,3,2,1,0:T(8,128)}, bf16[2,2,4,128,128]{4,3,2,1,0:T(8,128)(2,1)}) custom-call(s32[1]{0:T(128)} %bitcast.1.tile_ref, bf16[32,2,4,56,128]{4,3,2,1,0:T(8,128)(2,1)} %gather.1.msg_ref, f32[32,4,8,128]{3,2,1,0:T(8,128)} %constant.17.clone.tables_ref, bf16[256,256]{1,0:T(8,128)(2,1)} %constant.15.clone.right_ref, ...), custom_call_target="tpu_custom_call" | custom-call | tf_op jit(solution)/shard_map/grid/pallas_call | solution.py:347
  60.0 13.0 %exchange.1 = (bf16[2,4,128,128]{3,2,1,0:T(8,128)(2,1)}, bf16[2,4,128,128]{3,2,1,0:T(8,128)(2,1)}) custom-call(bf16[2,2,4,128,128]{4,3,2,1,0:T(8,128)(2,1)} %get-tuple-element.10.half_ref), custom_call_target="tpu_custom_call" | custom-call | tf_op jit(solution)/shard_map/exchange/pallas_call | solution.py:400
  72.9 3.6 %variation.1 = f32[2,2,4,128,128]{4,3,2,1,0:T(8,128)} custom-call(s32[1]{0:T(128)} %bitcast.frame_ref, f32[2,2,4,128,128]{4,3,2,1,0:T(8,128)} %get-tuple-element.9.half_ref, bf16[2,4,128,128]{3,2,1,0:T(8,128)(2,1)} %get-tuple-element.11.before_ref, bf16[2,4,128,128]{3,2,1,0:T(8,128)(2,1)} %get-tuple-element.12.after_ref), custom_call_target="tpu_custom_call" | custom-call | tf_op jit(solution)/shard_map/variation/pallas_call | solution.py:436

commit v3 on v2

--- a/solution.py
+++ b/solution.py
@@ -48,7 +48,7 @@
     return right.astype(np.float32), left.astype(np.float32)
 
 
-def message_kernel(samples_ref, density_ref, frac_ref, shift_ref, depth_ref, base_ref, out_ref, lines_ref):
+def write_message(samples_ref, density_ref, frac_ref, shift_ref, depth_ref, base_ref, out_ref, lines_ref):
     frames, blocks, channels, lanes = samples_ref.shape
     coils = channels // 2
     grid_mask = 127
@@ -82,20 +82,8 @@
     return np.stack([np.concatenate(pair, axis=1) for pair in pairs], axis=1).astype(np.float32)
 
 
-def block_messages(kspace_samples, density, sample_frac, row_offsets, depth_base, block_base):
-    frames, blocks, channels, lanes = kspace_samples.shape
-    vmem, smem = pl.BlockSpec(memory_space=pltpu.VMEM), pl.BlockSpec(memory_space=pltpu.SMEM)
-    return pl.pallas_call(
-        message_kernel,
-        out_shape=jax.ShapeDtypeStruct((frames, blocks, ROWS, lanes), jnp.bfloat16),
-        in_specs=[vmem] * 5 + [smem],
-        out_specs=vmem,
-        scratch_shapes=[pltpu.VMEM((frames * blocks, channels, lanes), jnp.float32)],
-        name="message",
-    )(kspace_samples, density, jnp.swapaxes(sample_frac, 1, 2), row_offsets, depth_base, jnp.swapaxes(block_base, 1, 2))
-
-
-def gather_kernel(side, msg_ref, out_ref, send_sem, recv_sem, own_sem):
+def gather_kernel(side, *refs):
+    *input_refs, out_ref, msg_ref, lines_ref, send_sem, recv_sem, own_sem = refs
     tile = lax.axis_index("tile")
     core, chip = tile % 2, tile // 2
     chip_x, chip_y = chip // side, chip % side
@@ -113,6 +101,7 @@
     barrier = pltpu.get_barrier_semaphore()
     for device in neighbours:
         pl.semaphore_signal(barrier, inc=1, device_id={"tile": device}, device_id_type=MESH)
+    write_message(*input_refs, msg_ref, lines_ref)
     pl.semaphore_wait(barrier, len(neighbours))
 
     copies = {}
@@ -220,25 +209,46 @@
     own.wait()
 
 
-def gather_messages(message, tiles, side):
+def gather_messages(kspace_samples, density, sample_frac, row_offsets, depth_base, block_base, tiles):
+    frames, blocks, channels, lanes = kspace_samples.shape
+    message = (frames, blocks, ROWS, lanes)
+    vmem, smem = pl.BlockSpec(memory_space=pltpu.VMEM), pl.BlockSpec(memory_space=pltpu.SMEM)
     return pl.pallas_call(
-        functools.partial(gather_kernel, side),
-        out_shape=jax.ShapeDtypeStruct((tiles,) + message.shape, message.dtype),
-        in_specs=[pl.BlockSpec(memory_space=pltpu.VMEM)],
+        functools.partial(gather_kernel, math.isqrt(tiles // 2)),
+        out_shape=jax.ShapeDtypeStruct((tiles,) + message, jnp.bfloat16),
+        in_specs=[vmem] * 5 + [smem],
         out_specs=pl.BlockSpec(memory_space=pl.ANY),
         scratch_shapes=[
+            pltpu.VMEM(message, jnp.bfloat16),
+            pltpu.VMEM((frames * blocks, channels, lanes), jnp.float32),
             pltpu.SemaphoreType.DMA((46,)),
             pltpu.SemaphoreType.DMA((46,)),
             pltpu.SemaphoreType.DMA(()),
         ],
         compiler_params=pltpu.CompilerParams(collective_id=0, has_side_effects=True),
         name="gather",
-    )(message)
-
-
-def grid_kernel(grid, coils, rows, blocks, scale, tile_ref, msg_ref, tables_ref, right_ref, left_ref, maps_ref, est_ref, out_ref, sent_ref, acc_ref, steps_ref):
-    here = tile_ref[0]
+    )(kspace_samples, density, jnp.swapaxes(sample_frac, 1, 2), row_offsets, depth_base, jnp.swapaxes(block_base, 1, 2))
+
+
+def grid_kernel(grid, coils, rows, blocks, scale, tile_ref, msg_hbm, tables_hbm, right_ref, left_ref, maps_hbm, est_hbm, out_ref, sent_ref, acc_ref, steps_ref, lines_ref, msg_ref, tables_ref, maps_ref, est_ref, msg_sem, tables_sem, maps_sem, est_sem):
+    frame = pl.program_id(0)
     half_rows = rows * coils
+
+    def message_copy(which):
+        return pltpu.make_async_copy(msg_hbm.at[:, which], msg_ref.at[which], msg_sem.at[which])
+
+    tables_copy = pltpu.make_async_copy(tables_hbm.at[tile_ref[0]], tables_ref, tables_sem)
+    maps_copy = pltpu.make_async_copy(maps_hbm, maps_ref, maps_sem)
+    est_copy = pltpu.make_async_copy(est_hbm, est_ref, est_sem)
+
+    @pl.when(frame == 0)
+    def _():
+        tables_copy.start()
+        for which in range(2):
+            message_copy(which).start()
+        maps_copy.start()
+        est_copy.start()
+
     plane = 2 * half_rows
     per_tile = msg_ref.shape[2]
     pitch = plane + 8
@@ -248,22 +258,27 @@
         return carry
 
     lax.fori_loop(0, grid * pitch // 128, clear, 0, unroll=4)
+    @pl.when(frame == 0)
+    def _():
+        tables_copy.wait()
+
+    message_copy(frame).wait()
     for tap in range(TAPS):
-        steps_ref[tap] = jnp.broadcast_to(tables_ref[here, 2][:, tap : tap + 1], (2 * rows, 128))
-        steps_ref[TAPS + tap] = jnp.broadcast_to(tables_ref[here, 3][:, tap : tap + 1], (2 * rows, 128))
+        steps_ref[tap] = jnp.broadcast_to(tables_ref[2][:, tap : tap + 1], (2 * rows, 128))
+        steps_ref[TAPS + tap] = jnp.broadcast_to(tables_ref[3][:, tap : tap + 1], (2 * rows, 128))
     cells = lax.broadcasted_iota(jnp.int32, (8, 128), 0)
 
     def one_block(block, carry):
         tile, local = block // per_tile, block % per_tile
-        real = msg_ref[tile, 0, local, 0:coils, :].astype(jnp.float32)
-        imag = msg_ref[tile, 0, local, coils : 2 * coils, :].astype(jnp.float32)
-        weights = msg_ref[tile, 0, local, ROW_WX : ROW_WX + 8, :].astype(jnp.float32)
-        depth = msg_ref[tile, 0, local, ROW_WZ : ROW_WZ + 8, :].astype(jnp.float32)
-        tail = msg_ref[tile, 0, local, ROW_WY : ROW_WY + 8, :].astype(jnp.float32)
+        real = msg_ref[frame, tile, local, 0:coils, :].astype(jnp.float32)
+        imag = msg_ref[frame, tile, local, coils : 2 * coils, :].astype(jnp.float32)
+        weights = msg_ref[frame, tile, local, ROW_WX : ROW_WX + 8, :].astype(jnp.float32)
+        depth = msg_ref[frame, tile, local, ROW_WZ : ROW_WZ + 8, :].astype(jnp.float32)
+        tail = msg_ref[frame, tile, local, ROW_WY : ROW_WY + 8, :].astype(jnp.float32)
         first_row = jnp.broadcast_to(tail[ROW_YB - ROW_WY : ROW_YB - ROW_WY + 1, :].astype(jnp.int32), (8, 128))
         first_cell = tail[ROW_ZB - ROW_WY : ROW_ZB - ROW_WY + 1, :].astype(jnp.int32)
-        turn = jnp.take_along_axis(tables_ref[here, 0], first_row, axis=1)
-        swapped = jnp.take_along_axis(tables_ref[here, 1], first_row, axis=1)
+        turn = jnp.take_along_axis(tables_ref[0], first_row, axis=1)
+        swapped = jnp.take_along_axis(tables_ref[1], first_row, axis=1)
         sum_same = sum(tail[e : e + 1] * steps_ref[e] for e in range(TAPS))
         sum_cross = sum(tail[e : e + 1] * steps_ref[TAPS + e] for e in range(TAPS))
         phase = turn * sum_same + swapped * sum_cross
@@ -294,25 +309,36 @@
 
     lax.fori_loop(0, blocks, one_block, 0, unroll=32)
 
+    @pl.when(frame == 0)
+    def _():
+        maps_copy.wait()
+        est_copy.wait()
+
     right = right_ref[...]
     left = left_ref[...]
     for y in range(rows):
         out_ref[0, 0, y] = jnp.zeros((grid, grid), jnp.float32)
         out_ref[0, 1, y] = jnp.zeros((grid, grid), jnp.float32)
 
-        def one_pair(pair, carry, y=y):
-            coil = pair * 2
+        for group in range(0, coils, 4):
             lines = []
-            for part in range(2):
-                base = y * coils + coil + part
+            for coil in range(group, group + 4):
+                base = y * coils + coil
                 re = acc_ref[pl.ds(base, grid, stride=pitch), :]
                 im = acc_ref[pl.ds(half_rows + base, grid, stride=pitch), :]
                 lines.append(jnp.concatenate([re, im], axis=1).astype(jnp.bfloat16))
-            second = jnp.dot(jnp.concatenate(lines, axis=0), right, preferred_element_type=jnp.float32).astype(jnp.bfloat16)
+            lines_ref[group * grid : (group + 4) * grid] = jnp.dot(
+                jnp.concatenate(lines, axis=0), right, preferred_element_type=jnp.float32
+            ).astype(jnp.bfloat16)
+
+        def one_pair(pair, carry, y=y):
+            coil = pair * 2
+            first_line = pl.multiple_of(coil * grid, 2 * grid)
+            one, two = lines_ref[pl.ds(first_line, grid)], lines_ref[pl.ds(first_line + grid, grid)]
             stacked = jnp.concatenate(
                 [
-                    jnp.concatenate([second[:grid, :grid], second[grid:, :grid]], axis=1),
-                    jnp.concatenate([second[:grid, grid:], second[grid:, grid:]], axis=1),
+                    jnp.concatenate([one[:, :grid], two[:, :grid]], axis=1),
+                    jnp.concatenate([one[:, grid:], two[:, grid:]], axis=1),
                 ],
                 axis=0,
             )
@@ -332,7 +358,7 @@
 
         lax.fori_loop(0, coils // 2, one_pair, 0, unroll=8)
         for part in range(2):
-            half = est_ref[0, part, y] + scale * out_ref[0, part, y]
+            half = est_ref[frame, part, y] + scale * out_ref[0, part, y]
             out_ref[0, part, y] = half
             sent_ref[0, part, y] = half.astype(jnp.bfloat16)
 
@@ -343,7 +369,7 @@
     blocks = tiles * per_tile
     right, left = (jnp.asarray(table, jnp.bfloat16) for table in dft_tables(grid))
     tables = jnp.asarray(row_tables(rows, grid, gathered.shape[-1]))
-    once = pl.Buffered(1)
+    once, anywhere = pl.Buffered(1), pl.BlockSpec(memory_space=pl.ANY)
     return pl.pallas_call(
         functools.partial(grid_kernel, grid, coils, rows, blocks, scale),
         out_shape=[jax.ShapeDtypeStruct(estimate.shape, kind) for kind in (jnp.float32, jnp.bfloat16)],
@@ -351,17 +377,26 @@
             num_scalar_prefetch=1,
             grid=(frames,),
             in_specs=[
-                pl.BlockSpec((tiles, 1, per_tile, ROWS, 128), lambda f, s: (0, f, 0, 0, 0)),
-                pl.BlockSpec(tables.shape, lambda f, s: (0, 0, 0, 0), pipeline_mode=once),
+                anywhere,
+                anywhere,
                 pl.BlockSpec((2 * grid, 2 * grid), lambda f, s: (0, 0), pipeline_mode=once),
                 pl.BlockSpec((2 * grid, 2 * grid), lambda f, s: (0, 0), pipeline_mode=once),
-                pl.BlockSpec(coil_maps.shape, lambda f, s: (0, 0, 0, 0, 0), pipeline_mode=once),
-                pl.BlockSpec((1, 2, rows, grid, grid), lambda f, s: (f, 0, 0, 0, 0)),
+                anywhere,
+                anywhere,
             ],
             out_specs=[pl.BlockSpec((1, 2, rows, grid, grid), lambda f, s: (f, 0, 0, 0, 0))] * 2,
             scratch_shapes=[
                 pltpu.VMEM((grid * (2 * rows * coils + 8), grid), jnp.float32),
                 pltpu.VMEM((2 * TAPS, 2 * rows, 128), jnp.float32),
+                pltpu.VMEM((coils * grid, 2 * grid), jnp.bfloat16),
+                pltpu.VMEM((frames, tiles, per_tile, ROWS, 128), gathered.dtype),
+                pltpu.VMEM(tables.shape[1:], tables.dtype),
+                pltpu.VMEM(coil_maps.shape, coil_maps.dtype),
+                pltpu.VMEM(estimate.shape, estimate.dtype),
+                pltpu.SemaphoreType.DMA((frames,)),
+                pltpu.SemaphoreType.DMA(()),
+                pltpu.SemaphoreType.DMA(()),
+                pltpu.SemaphoreType.DMA(()),
             ],
         ),
         compiler_params=pltpu.CompilerParams(vmem_limit_bytes=56 * 1024 * 1024),
@@ -416,28 +451,29 @@
         factor = lax.rsqrt(change[0] * change[0] + change[1] * change[1] + EPS * EPS)
         return [change[part] * factor for part in range(2)]
 
-    first = [half_ref[0, part, 0] for part in range(2)]
-    last = [half_ref[1, part, 0] for part in range(2)]
-    before = [before_ref[part, 0].astype(jnp.float32) for part in range(2)]
-    after = [after_ref[part, 0].astype(jnp.float32) for part in range(2)]
-    psi_before, psi_here, psi_after = psi(first, before), psi(last, first), psi(after, last)
-    for part in range(2):
-        low = jnp.where(here > 0, psi_before[part], 0.0)
-        high = jnp.where(here < count - 1, psi_after[part], 0.0)
-        out_ref[0, part, 0] = first[part] - LAMBDA_TV * (low - psi_here[part])
-        out_ref[1, part, 0] = last[part] - LAMBDA_TV * (psi_here[part] - high)
+    for y in range(half_ref.shape[2]):
+        first = [half_ref[0, part, y] for part in range(2)]
+        last = [half_ref[1, part, y] for part in range(2)]
+        before = [before_ref[part, y].astype(jnp.float32) for part in range(2)]
+        after = [after_ref[part, y].astype(jnp.float32) for part in range(2)]
+        psi_before, psi_here, psi_after = psi(first, before), psi(last, first), psi(after, last)
+        for part in range(2):
+            low = jnp.where(here > 0, psi_before[part], 0.0)
+            high = jnp.where(here < count - 1, psi_after[part], 0.0)
+            out_ref[0, part, y] = first[part] - LAMBDA_TV * (low - psi_here[part])
+            out_ref[1, part, y] = last[part] - LAMBDA_TV * (psi_here[part] - high)
 
 
 def variation_step(half, before, after, frame_here, count):
     frames, parts, rows, grid, _ = half.shape
     assert frames == 2
-    whole = pl.BlockSpec((frames, parts, 1, grid, grid), lambda y, s: (0, 0, y, 0, 0))
-    side = pl.BlockSpec((parts, 1, grid, grid), lambda y, s: (0, y, 0, 0))
+    whole = pl.BlockSpec((frames, parts, rows // 2, grid, grid), lambda y, s: (0, 0, y, 0, 0))
+    side = pl.BlockSpec((parts, rows // 2, grid, grid), lambda y, s: (0, y, 0, 0))
     return pl.pallas_call(
         functools.partial(variation_kernel, count),
         out_shape=jax.ShapeDtypeStruct(half.shape, half.dtype),
         grid_spec=pltpu.PrefetchScalarGridSpec(
-            num_scalar_prefetch=1, grid=(rows,), in_specs=[whole, side, side], out_specs=whole
+            num_scalar_prefetch=1, grid=(2,), in_specs=[whole, side, side], out_specs=whole
         ),
         name="variation",
     )(frame_here, half, before, after)
@@ -455,9 +491,9 @@
     rows = coil_maps.shape[2]
     scale = 1.0 / (8.0 * math.sqrt(per_tile * tile_count * samples))
 
-    message = block_messages(kspace_samples, density, sample_frac, row_offsets, depth_base, block_base)
-    gathered = gather_messages(message, tile_count, math.isqrt(tile_count // 2))
-
+    gathered = gather_messages(
+        kspace_samples, density, sample_frac, row_offsets, depth_base, block_base, tile_count
+    )
     half, rounded = half_step(gathered, tile_here.reshape(1), coil_maps, estimate, scale)
     before, after = exchange_frames(rounded, lax.axis_size("frame"))
     return variation_step(half, before, after, frame_here.reshape(1), lax.axis_size("frame"))

time: 76.7 us -> 72.4 us (0.944)
  Pallas kernels: 76.5 us -> 72.1 us
    pallas_call x2 -> x1, Pallas kernels: 25.4 us -> 23.5 us  [gather_messages(): pl.pallas_call(functools.partial(gather_kernel, math.isqrt(tiles // 2)),...]
    pallas_call x1, Pallas kernels: 34.6 us -> 33.1 us  [half_step(): pl.pallas_call(functools.partial(grid_kernel, grid, coils, rows, blocks,...]
    pallas_call x1, Pallas kernels: 3.57 us -> 2.37 us  [variation_step(): pl.pallas_call(functools.partial(variation_kernel, count), out_shape=jax....]
where the time goes in v3:
time: 72.4 us; the launch traced here: 72.2 us
  Pallas kernels  72.1 us (100%)
    pallas_call x1, Pallas kernels, half_step(): pl.pallas_call(functools.partial(grid_kernel, grid, coils, rows, blocks,...  33.1 us
    pallas_call x1, Pallas kernels, gather_messages(): pl.pallas_call(functools.partial(gather_kernel, math.isqrt(tiles // 2)),...  23.5 us
    pallas_call x1, Pallas kernels, exchange_frames(): pl.pallas_call(functools.partial(exchange_kernel, count), out_shape=[jax....  13.1 us
    pallas_call x1, Pallas kernels, variation_step(): pl.pallas_call(functools.partial(variation_kernel, count), out_shape=jax....  2.37 us

profile of v3, /device:TPU:1, one launch (start us, length us, event | category | flops | bytes accessed | tf_op | source)
XLA Modules:
  0.0 72.2 jit_solution(8551724388644566654)
XLA Ops:
  0.0 23.5 %gather.1.msg_hbm = bf16[32,2,4,56,128]{4,3,2,1,0:T(8,128)(2,1)} custom-call(bf16[2,4,32,128]{3,2,1,0:T(8,128)(2,1)} %refs_0_.1, bf16[2,4,128]{2,1,0:T(4,128)(2,1)} %refs_1_.1, bf16[2,3,4,128]{3,2,1,0:T(4,128)(2,1)} %bitcast.4, s32[2,4,128]{2,1,0:T(4,128)} %refs_3_.1, s32[2,4,128]{2,1,0:T(4,128)} %refs_4_.1, s32[2,2,4]{2,1,0:T(2,128)} %bitcast.5), custom_call_target="tpu_custom_call" | custom-call | tf_op jit(solution)/shard_map/gather/pallas_call | solution.py:216
  23.5 33.1 %grid.1 = (f32[2,2,4,128,128]{4,3,2,1,0:T(8,128)}, bf16[2,2,4,128,128]{4,3,2,1,0:T(8,128)(2,1)}) custom-call(s32[1]{0:T(128)} %bitcast.1.tile_ref, bf16[32,2,4,56,128]{4,3,2,1,0:T(8,128)(2,1)} %gather.1.msg_hbm, f32[32,4,8,128]{3,2,1,0:T(8,128)} %constant.17.clone.tables_hbm, bf16[256,256]{1,0:T(8,128)(2,1)} %constant.15.clone.right_ref, ...), custom_call_target="tpu_custom_call" | custom-call | tf_op jit(solution)/shard_map/grid/pallas_call | solution.py:373
  56.7 13.1 %exchange.1 = (bf16[2,4,128,128]{3,2,1,0:T(8,128)(2,1)}, bf16[2,4,128,128]{3,2,1,0:T(8,128)(2,1)}) custom-call(bf16[2,2,4,128,128]{4,3,2,1,0:T(8,128)(2,1)} %get-tuple-element.10.half_ref), custom_call_target="tpu_custom_call" | custom-call | tf_op jit(solution)/shard_map/exchange/pallas_call | solution.py:435
  69.8 2.4 %variation.1 = f32[2,2,4,128,128]{4,3,2,1,0:T(8,128)} custom-call(s32[1]{0:T(128)} %bitcast.frame_ref, f32[2,2,4,128,128]{4,3,2,1,0:T(8,128)} %get-tuple-element.9.half_ref, bf16[2,4,128,128]{3,2,1,0:T(8,128)(2,1)} %get-tuple-element.11.before_ref, bf16[2,4,128,128]{3,2,1,0:T(8,128)(2,1)} %get-tuple-element.12.after_ref), custom_call_target="tpu_custom_call" | custom-call | tf_op jit(solution)/shard_map/variation/pallas_call | solution.py:472

commit v4 on v3

--- a/solution.py
+++ b/solution.py
@@ -96,7 +96,7 @@
         return ((first + along + side) % side) * first_step + ((other + across + side) % side) * other_step + core
 
     partner = tile + 1 - 2 * core
-    neighbours = [at(1, 0), at(-1, 0), at(0, 1), at(0, -1), partner]
+    neighbours = [at(1, 0), at(-1, 0), at(2, 0), at(0, 1), at(0, -1), at(0, 2), partner]
 
     barrier = pltpu.get_barrier_semaphore()
     for device in neighbours:
@@ -121,14 +121,18 @@
     for frame in (0, 1):
         for way in (1, -1):
             make(("first", 0, frame, way), tile, frame, at(way, 0), True)
-    make(("pass", 0), at(-1, 0), 0, at(1, 0), False)
-    make(("pass", 1), at(1, 0), 1, at(-1, 0), False)
+    make(("pass", 0), tile, 0, at(2, 0), True)
+    make(("pass", 1), tile, 1, at(2, 0), True)
     for along in (0, -1, 1, 2):
         for frame in (0, 1):
             for way in (1, -1):
                 make(("second", along, frame, way), at(along, 0), frame, at(0, way), along == 0)
-        make(("hand", along, 0), at(along, -1), 0, at(0, 1), False)
-        make(("hand", along, 1), at(along, 1), 1, at(0, -1), False)
+        for frame in (0, 1):
+            way = 1 - 2 * frame
+            if along == 2:
+                make(("hand", along, frame), at(along, 0), frame, at(0, 2), along == 0)
+            else:
+                make(("hand", along, frame), at(along, -way), frame, at(0, way), False)
         for across in (0, -1, 1, 2):
             make(("core", along, across), at(along, across), None, partner, along == 0 and across == 0)
 
@@ -144,6 +148,8 @@
         for frame in frames:
             way = 1 - 2 * frame
             start(("second", along, frame, way), ("second", along, frame, -way))
+            if along == 2:
+                start(("hand", along, frame))
 
     there = {}
 
@@ -153,16 +159,14 @@
             start(("core", along, across))
 
     own = pltpu.make_async_copy(msg_ref, out_ref.at[tile], own_sem)
-    start(("first", 0, 0, 1), ("first", 0, 1, -1), ("first", 0, 1, 1), ("first", 0, 0, -1))
+    start(("first", 0, 0, 1), ("first", 0, 1, -1), ("first", 0, 1, 1), ("first", 0, 0, -1), ("pass", 0), ("pass", 1))
     second(0, 0, 1)
     own.start()
     to_core(0, 0, 0, 1)
     arrived(("first", 0, 0, 1))
-    start(("pass", 0))
     second(-1, 0)
     to_core(-1, 0, 0)
     arrived(("first", 0, 1, -1))
-    start(("pass", 1))
     second(1, 1)
     to_core(1, 0, 1)
     arrived(("first", 0, 1, 1))
@@ -192,7 +196,8 @@
         for frame in order:
             way = 1 - 2 * frame
             arrived(("second", along, frame, way))
-            start(("hand", along, frame))
+            if along != 2:
+                start(("hand", along, frame))
             to_core(along, -way, frame)
         for frame in order:
             way = 1 - 2 * frame
@@ -307,7 +312,7 @@
             acc_ref[pl.ds(start, plane), :] += value[tap * plane : (tap + 1) * plane]
         return carry
 
-    lax.fori_loop(0, blocks, one_block, 0, unroll=32)
+    lax.fori_loop(0, blocks, one_block, 0, unroll=64)
 
     @pl.when(frame == 0)
     def _():

time: 72.4 us -> 71 us (0.981)
  Pallas kernels: 72.1 us -> 70.8 us
where the time goes in v4:
time: 71 us; the launch traced here: 70.8 us
  Pallas kernels  70.8 us (100%)
    pallas_call x1, Pallas kernels, half_step(): pl.pallas_call(functools.partial(grid_kernel, grid, coils, rows, blocks,...  32.5 us
    pallas_call x1, Pallas kernels, gather_messages(): pl.pallas_call(functools.partial(gather_kernel, math.isqrt(tiles // 2)),...  22.8 us
    pallas_call x1, Pallas kernels, exchange_frames(): pl.pallas_call(functools.partial(exchange_kernel, count), out_shape=[jax....  13.1 us
    pallas_call x1, Pallas kernels, variation_step(): pl.pallas_call(functools.partial(variation_kernel, count), out_shape=jax....  2.37 us

profile of v4, /device:TPU:1, one launch (start us, length us, event | category | flops | bytes accessed | tf_op | source)
XLA Modules:
  0.0 70.8 jit_solution(3302606051376050643)
XLA Ops:
  0.0 22.8 %gather.1.msg_hbm = bf16[32,2,4,56,128]{4,3,2,1,0:T(8,128)(2,1)} custom-call(bf16[2,4,32,128]{3,2,1,0:T(8,128)(2,1)} %refs_0_.1, bf16[2,4,128]{2,1,0:T(4,128)(2,1)} %refs_1_.1, bf16[2,3,4,128]{3,2,1,0:T(4,128)(2,1)} %bitcast.4, s32[2,4,128]{2,1,0:T(4,128)} %refs_3_.1, s32[2,4,128]{2,1,0:T(4,128)} %refs_4_.1, s32[2,2,4]{2,1,0:T(2,128)} %bitcast.5), custom_call_target="tpu_custom_call" | custom-call | tf_op jit(solution)/shard_map/gather/pallas_call | solution.py:221
  22.8 32.5 %grid.1 = (f32[2,2,4,128,128]{4,3,2,1,0:T(8,128)}, bf16[2,2,4,128,128]{4,3,2,1,0:T(8,128)(2,1)}) custom-call(s32[1]{0:T(128)} %bitcast.1.tile_ref, bf16[32,2,4,56,128]{4,3,2,1,0:T(8,128)(2,1)} %gather.1.msg_hbm, f32[32,4,8,128]{3,2,1,0:T(8,128)} %constant.17.clone.tables_hbm, bf16[256,256]{1,0:T(8,128)(2,1)} %constant.15.clone.right_ref, ...), custom_call_target="tpu_custom_call" | custom-call | tf_op jit(solution)/shard_map/grid/pallas_call | solution.py:378
  55.3 13.1 %exchange.1 = (bf16[2,4,128,128]{3,2,1,0:T(8,128)(2,1)}, bf16[2,4,128,128]{3,2,1,0:T(8,128)(2,1)}) custom-call(bf16[2,2,4,128,128]{4,3,2,1,0:T(8,128)(2,1)} %get-tuple-element.10.half_ref), custom_call_target="tpu_custom_call" | custom-call | tf_op jit(solution)/shard_map/exchange/pallas_call | solution.py:440
  68.4 2.4 %variation.1 = f32[2,2,4,128,128]{4,3,2,1,0:T(8,128)} custom-call(s32[1]{0:T(128)} %bitcast.frame_ref, f32[2,2,4,128,128]{4,3,2,1,0:T(8,128)} %get-tuple-element.9.half_ref, bf16[2,4,128,128]{3,2,1,0:T(8,128)(2,1)} %get-tuple-element.11.before_ref, bf16[2,4,128,128]{3,2,1,0:T(8,128)(2,1)} %get-tuple-element.12.after_ref), custom_call_target="tpu_custom_call" | custom-call | tf_op jit(solution)/shard_map/variation/pallas_call | solution.py:477
